TPU v7x, 512 devices: a whole 4x8x8 slice. The times are simulated.
512 devices in a mesh: leaf: 32 (over x, y), front: 16 (over z, core).
Axes of the slice: x: 4, y: 8, z: 8, core: 2. Of those that a mesh axis runs over, the one named last changes fastest.
Arguments:
- child_pivot: float32 [32, 512, 512], P('leaf', 'front')
- child_panel: float32 [32, 2048, 512], P('leaf', 'front'), may hold values from -0.9 to 0.9
- anc_front: float32 [32, 16, 512, 512], P('leaf', 'front')
- dest_list: int32 [32, 16], replicated, may hold values from 0 to 31, as said below
- col_list: int32 [32, 16], replicated, may hold values from 0 to 3, as said below
- row_list: int32 [32, 16], replicated, may hold values from 0 to 3, as said below
Outputs:
- child_lower: float32 [32, 512, 512], P('leaf', 'front')
- child_factor: float32 [32, 2048, 512], P('leaf', 'front')
- anc_factor: float32 [32, 16, 512, 512], P('leaf', 'front')
Inputs may be any that keep to these rules, and one draw needn't show every extreme that they name: dest_list[g, j] is g with exactly one bit of its index flipped; every group that row g names is named there by exactly 4 column blocks, so row g names 4 different groups. `col_list`: column blocks of one group that name the same group in dest_list have different entries here. row_list[g, f] is 1 or more for f < 4.
All inputs are finite; a program needn't handle non-finite values.
Results may differ from a plain program's by a relative error of at most 0.0001.
Values sent between devices are 32-bit elements; how exact they have to be, the bound alone decides.
No kernel may reach another device: no remote copies, remote signals or barrier semaphores. Data moves between devices by JAX's collectives and lax.ppermute only.
A program may use at most 64 MiB of HBM per device.

v0:
```python
import jax
import jax.numpy as jnp
from jax import lax
from jax.sharding import PartitionSpec as P


def swapped(value, axis, distance):
    mask = 2**distance
    pairs = [(source, source ^ mask) for source in range(lax.axis_size(axis))]
    return lax.ppermute(value, axis, pairs)


def schur_block(left, right):
    return lax.dot_general(
        left,
        right,
        (((1,), (1,)), ((), ())),
        precision=lax.Precision.HIGHEST,
        preferred_element_type=jnp.float32,
    )


def slot_ranks(dest_list):
    count = dest_list.shape[1]
    positions = jnp.arange(count, dtype=jnp.int32)
    earlier = positions[:, None] > positions[None, :]
    same = dest_list[:, :, None] == dest_list[:, None, :]
    return jnp.sum((same & earlier[None]).astype(jnp.int32), axis=2)


def lookup_rows(table, sender_ids):
    leaf_ids = jnp.arange(table.shape[0], dtype=jnp.int32)
    hits = (sender_ids[:, None] == leaf_ids[None, :]).astype(jnp.int32)
    return jnp.sum(hits[:, :, None] * table[None], axis=1)


def pick_blocks(own_targets, own_ranks, target, slot_ids, update_blocks):
    select = ((own_targets[None, :] == target) & (own_ranks[None, :] == slot_ids[:, None])).astype(
        jnp.float32
    )
    return jnp.einsum("kj,xjy->kxy", select, update_blocks, precision=lax.Precision.HIGHEST)


def per_device(child_pivot, child_panel, anc_front, dest_list, col_list, row_list):
    front_count = lax.axis_size("front")
    front_pos = lax.axis_index("front")
    group = lax.axis_index("leaf")
    slab = child_pivot.shape[1]
    block = child_panel.shape[1]
    width = child_panel.shape[2]
    blocks_wide = width // block
    row_slots = anc_front.shape[2] // block
    pivot = lax.all_gather(child_pivot[0], "front", axis=0, tiled=True)
    lower = jnp.linalg.cholesky(pivot)
    lower_rows = lax.dynamic_slice_in_dim(lower, front_pos * slab, slab, 0)
    panel = lax.linalg.triangular_solve(
        lower, child_panel[0], left_side=False, lower=True, transpose_a=True
    )
    update = schur_block(panel, lax.all_gather(panel, "front", axis=0, tiled=True))
    ranks = slot_ranks(dest_list)
    slot_ids = jnp.arange(blocks_wide, dtype=jnp.int32)
    own_targets = lax.dynamic_index_in_dim(dest_list, group, 0, keepdims=False)
    own_ranks = lax.dynamic_index_in_dim(ranks, group, 0, keepdims=False)
    update_blocks = update.reshape(block, front_count, block)
    levels = lax.axis_size("leaf").bit_length() - 1
    arrived = []
    partners = []
    for level_bit in range(levels):
        partner = jnp.bitwise_xor(group, 1 << level_bit)
        outgoing = pick_blocks(own_targets, own_ranks, partner, slot_ids, update_blocks)
        arrived.append(swapped(outgoing, "leaf", level_bit))
        partners.append(partner)
    received = jnp.stack(arrived)
    sender_ids = jnp.stack(partners)
    src_dest = lookup_rows(dest_list, sender_ids)
    src_ranks = lookup_rows(ranks, sender_ids)
    src_cols = lookup_rows(col_list, sender_ids)
    src_rows = lookup_rows(row_list, sender_ids)
    match = (src_dest == group)[:, None, :] & (src_ranks[:, None, :] == slot_ids[None, :, None])
    live = jnp.sum(match.astype(jnp.int32), axis=2)
    column_of = jnp.sum(jnp.where(match, src_cols[:, None, :], 0), axis=2)
    row_of = lax.dynamic_index_in_dim(src_rows, front_pos, 1, keepdims=False)
    slot_rows = jnp.arange(row_slots, dtype=jnp.int32)
    slot_cols = jnp.arange(blocks_wide, dtype=jnp.int32)
    weight = (
        (live[:, :, None, None] == 1)
        & (row_of[:, None, None, None] == slot_rows[None, None, :, None])
        & (column_of[:, :, None, None] == slot_cols[None, None, None, :])
    ).astype(jnp.float32)
    incoming = jnp.einsum("gkrc,gkxy->rxcy", weight, received, precision=lax.Precision.HIGHEST)
    assembled = anc_front[0, 0] - incoming.reshape(row_slots * block, width)
    owner = front_pos < blocks_wide
    owner_pos = jnp.minimum(front_pos, blocks_wide - 1)
    top_rows = jnp.where(owner, assembled[:block], 0.0)
    contribution = lax.dynamic_update_slice_in_dim(
        jnp.zeros((width, width), jnp.float32), top_rows, owner_pos * block, 0
    )
    anc_pivot = lax.psum(contribution, "front")
    anc_lower = jnp.linalg.cholesky(anc_pivot)
    solved = lax.linalg.triangular_solve(
        anc_lower, assembled, left_side=False, lower=True, transpose_a=True
    )
    own_lower = lax.dynamic_slice_in_dim(anc_lower, owner_pos * block, block, 0)
    padded = lax.dynamic_update_slice_in_dim(jnp.zeros_like(solved), own_lower, 0, 0)
    row_ids = jnp.arange(row_slots * block, dtype=jnp.int32)
    mask = (row_ids < block)[:, None] & owner
    anc_out = jnp.where(mask, padded, solved)
    return (lower_rows[None], panel[None], anc_out[None, None])


def solution(mesh):
    in_specs = (
        P("leaf", "front", None),
        P("leaf", "front", None),
        P("leaf", "front", None, None),
        P(),
        P(),
        P(),
    )
    out_specs = (P("leaf", "front", None), P("leaf", "front", None), P("leaf", "front", None, None))
    return jax.shard_map(
        per_device, mesh=mesh, in_specs=in_specs, out_specs=out_specs, check_vma=False
    )
```

profile of v0, /device:TPU:1, one launch (start us, length us, event | category | flops | bytes accessed | tf_op | source)
XLA Modules:
  0.0 557.9 jit_solution(7262948002128751580)
XLA Ops:
  7.2 1.5 copy.131
  8.8 49.6 %all-gather.6.cloned.1.call-done = f32[1,512,512]{2,0,1:T(1,128)} async-done(((f32[1,32,512]{2,0,1:T(1,128)}), f32[1,512,512]{2,0,1:T(1,128)}) %all-gather.6.cloned.1.call-update) | async-done | bytes 1048592 | tf_op jit(solution)/shard_map/all_gather | solution.py:53
  58.5 2.4 copy.132
  61.2 11.7 %cholesky.286 = f32[128,128]{1,0:T(8,128)S(1)} custom-call(f32[128,128]{1,0:T(8,128)S(1)} %cholesky.426), custom_call_target="Cholesky" | custom-call | tf_op jit(solution)/shard_map/jit(cholesky)/cholesky | solution.py:54
  73.0 9.8 %custom-call.31 = f32[1,128,128]{1,2,0:T(8,128)S(1)} custom-call(f32[1,128,128]{2,1,0:T(8,128)S(1)} %get-tuple-element.123), custom_call_target="InvertDiagBlocksLowerTriangular" | custom-call | tf_op jit(solution)/shard_map/jit(cholesky)/cholesky | solution.py:54
  83.6 11.7 %cholesky.305 = f32[128,128]{1,0:T(8,128)S(1)} custom-call(f32[128,128]{1,0:T(8,128)S(1)} %cholesky.430), custom_call_target="Cholesky" | custom-call | tf_op jit(solution)/shard_map/jit(cholesky)/cholesky | solution.py:54
  95.5 10.0 %custom-call.32 = f32[1,128,128]{1,2,0:T(8,128)S(1)} custom-call(f32[1,128,128]{2,1,0:T(8,128)S(1)} %get-tuple-element.121), custom_call_target="InvertDiagBlocksLowerTriangular" | custom-call | tf_op jit(solution)/shard_map/jit(cholesky)/cholesky | solution.py:54
  106.6 11.7 %cholesky.326 = f32[128,128]{1,0:T(8,128)S(1)} custom-call(f32[128,128]{1,0:T(8,128)S(1)} %cholesky.435), custom_call_target="Cholesky" | custom-call | tf_op jit(solution)/shard_map/jit(cholesky)/cholesky | solution.py:54
  118.4 9.8 %custom-call.33 = f32[1,128,128]{1,2,0:T(8,128)S(1)} custom-call(f32[1,128,128]{2,1,0:T(8,128)S(1)} %get-tuple-element.119), custom_call_target="InvertDiagBlocksLowerTriangular" | custom-call | tf_op jit(solution)/shard_map/jit(cholesky)/cholesky | solution.py:54
  129.1 12.1 %cholesky.343 = f32[128,128]{1,0:T(8,128)S(1)} custom-call(f32[128,128]{1,0:T(8,128)S(1)} %convolution_subtract_fusion.11), custom_call_target="Cholesky" | custom-call | tf_op jit(solution)/shard_map/jit(cholesky)/cholesky | solution.py:54
  141.3 0.6 compare_reduce_fusion.10
  141.9 0.7 compare_reduce_fusion.9
  142.6 0.6 compare_reduce_fusion.11
  145.9 1.2 fusion.5
  147.2 8.5 %while.2 = (s32[]{:T(128)}, f32[512,512]{0,1:T(8,128)S(1)}, s32[4,2]{0,1:T(2,128)S(1)}, f32[4,128,128]{2,1,0:T(8,128)S(1)}, s32[]{:T(128)}) while((s32[]{:T(128)}, f32[512,512]{0,1:T(8,128)S(1)}, s32[4,2]{0,1:T(2,128)S(1)}, f32[4,128,128]{2,1,0:T(8,128)S(1)}, s32[]{:T(128)}) %tuple.71), condition=%wide.while_cond, body=%wide.while_body.sunk | while | flops 2 | bytes 393329 | solution.py:56
  147.8 1.4 dynamic-slice.13
  149.9 1.4 dynamic-slice.13
  152.0 1.4 dynamic-slice.13
  154.1 1.4 dynamic-slice.13
  155.6 39.3 %custom-call.26 = f32[4,128,128]{1,2,0:T(8,128)S(1)} custom-call(f32[4,128,128]{2,1,0:T(8,128)S(1)} %get-tuple-element.11), custom_call_target="InvertDiagBlocksLowerTriangular" | custom-call | tf_op jit(solution)/shard_map/triangular_solve | solution.py:56
  197.3 0.7 pad_maximum_fusion
  198.2 1.6 copy.143
  201.5 47.6 %all-gather.4.cloned.1.call-done = f32[2048,512]{0,1:T(8,128)} async-done(((f32[128,512]{0,1:T(8,128)}), f32[2048,512]{0,1:T(8,128)}) %all-gather.4.cloned.1.call-update) | async-done | bytes 4194320 | tf_op jit(solution)/shard_map/all_gather | solution.py:59
  249.1 4.5 convolution_bitcast_fusion
  254.3 2.6 collective-permute-start
  257.3 4.0 collective-permute-start.1
  261.9 4.4 collective-permute-start.2
  266.7 3.1 collective-permute-start.3
  270.3 4.5 collective-permute-start.4
  274.9 9.5 %collective-permute-done.1 = f32[4,128,128]{2,0,1:T(4,128)S(1)} collective-permute-done((f32[4,128,128]{2,0,1:T(4,128)S(1)}, f32[4,128,128]{2,0,1:T(4,128)S(1)}, u32[]{:S(2)}, u32[]{:S(2)}) %collective-permute-start.1) | collective-permute-done | bytes 262176 | tf_op jit(solution)/shard_map/ppermute | solution.py:10
  284.6 1.2 convolution_bitcast_fusion.1
  286.7 1.0 copy-done.2
  287.8 1.1 constant_dynamic-slice_fusion.3
  288.9 0.7 copy.141
  289.6 0.8 copy.158
  290.5 113.9 %all-reduce.4.cloned.1.call-done = f32[512,512]{0,1:T(8,128)} async-done(((f32[512,512]{0,1:T(8,128)}), f32[512,512]{0,1:T(8,128)}) %all-reduce.4.cloned.1.call-update) | async-done | bytes 1048592 | tf_op jit(solution)/shard_map/psum | solution.py:98
  404.4 1.6 copy.146
  406.3 1.0 copy-done.3
  407.3 11.7 %cholesky.358 = f32[128,128]{1,0:T(8,128)S(1)} custom-call(f32[128,128]{1,0:T(8,128)S(1)} %cholesky.439), custom_call_target="Cholesky" | custom-call | tf_op jit(solution)/shard_map/jit(cholesky)/cholesky | solution.py:99
  419.1 9.8 %custom-call.34 = f32[1,128,128]{1,2,0:T(8,128)S(1)} custom-call(f32[1,128,128]{2,1,0:T(8,128)S(1)} %get-tuple-element.117), custom_call_target="InvertDiagBlocksLowerTriangular" | custom-call | tf_op jit(solution)/shard_map/jit(cholesky)/cholesky | solution.py:99
  428.9 1.2 fusion.21
  430.3 1.3 convolution_subtract_fusion.3
  431.6 11.9 %cholesky.377 = f32[128,128]{1,0:T(8,128)S(1)} custom-call(f32[128,128]{1,0:T(8,128)S(1)} %cholesky.443), custom_call_target="Cholesky" | custom-call | tf_op jit(solution)/shard_map/jit(cholesky)/cholesky | solution.py:99
  443.6 9.8 %custom-call.35 = f32[1,128,128]{1,2,0:T(8,128)S(1)} custom-call(f32[1,128,128]{2,1,0:T(8,128)S(1)} %get-tuple-element.115), custom_call_target="InvertDiagBlocksLowerTriangular" | custom-call | tf_op jit(solution)/shard_map/jit(cholesky)/cholesky | solution.py:99
  453.9 1.5 convolution_subtract_fusion.5
  455.4 11.7 %cholesky.398 = f32[128,128]{1,0:T(8,128)S(1)} custom-call(f32[128,128]{1,0:T(8,128)S(1)} %cholesky.448), custom_call_target="Cholesky" | custom-call | tf_op jit(solution)/shard_map/jit(cholesky)/cholesky | solution.py:99
  467.3 9.8 %custom-call.36 = f32[1,128,128]{1,2,0:T(8,128)S(1)} custom-call(f32[1,128,128]{2,1,0:T(8,128)S(1)} %get-tuple-element.113), custom_call_target="InvertDiagBlocksLowerTriangular" | custom-call | tf_op jit(solution)/shard_map/jit(cholesky)/cholesky | solution.py:99
  477.4 1.3 convolution_subtract_fusion.9
  478.8 12.0 %cholesky.415 = f32[128,128]{1,0:T(8,128)S(1)} custom-call(f32[128,128]{1,0:T(8,128)S(1)} %convolution_subtract_fusion.9), custom_call_target="Cholesky" | custom-call | tf_op jit(solution)/shard_map/jit(cholesky)/cholesky | solution.py:99
  490.9 0.6 compare_reduce_fusion.8
  491.5 0.7 compare_reduce_fusion.7
  492.2 0.6 compare_reduce_fusion.6
  492.8 0.7 compare_reduce_fusion.5
  496.0 1.2 fusion.4
  497.3 8.6 %while.3 = (s32[]{:T(128)}, f32[512,512]{0,1:T(8,128)S(1)}, s32[4,2]{0,1:T(2,128)S(1)}, f32[4,128,128]{2,1,0:T(8,128)S(1)}, s32[]{:T(128)}) while((s32[]{:T(128)}, f32[512,512]{0,1:T(8,128)S(1)}, s32[4,2]{0,1:T(2,128)S(1)}, f32[4,128,128]{2,1,0:T(8,128)S(1)}, s32[]{:T(128)}) %tuple.83), condition=%wide.while_cond.1, body=%wide.while_body.1.sunk | while | flops 2 | bytes 393329 | solution.py:100
  497.4 0.6 fusion.125
  498.0 1.3 dynamic-slice.15
  500.1 1.3 dynamic-slice.15
  502.3 1.3 dynamic-slice.15
  504.4 1.3 dynamic-slice.15
  505.9 39.3 %custom-call.27 = f32[4,128,128]{1,2,0:T(8,128)S(1)} custom-call(f32[4,128,128]{2,1,0:T(8,128)S(1)} %get-tuple-element.19), custom_call_target="InvertDiagBlocksLowerTriangular" | custom-call | tf_op jit(solution)/shard_map/triangular_solve | solution.py:100
  547.4 0.7 convolution_subtract_fusion.2
  548.5 1.0 constant_dynamic-slice_fusion.2
  549.6 1.3 copy.159
  (147 shorter events, 20.8 us)
Async XLA Ops:
  7.2 51.3 %all-gather.6.cloned.1.call-start = ((), (), s32[]{:S(2)}) async-start(), calls=%async_computation.2 | async-start | bytes 1114112 | tf_op jit(solution)/shard_map/all_gather | solution.py:53
  8.8 240.3 %all-gather.4.cloned.1.call-start = ((), (), s32[]{:S(2)}) async-start(), calls=%async_computation | async-start | bytes 4456448 | tf_op jit(solution)/shard_map/all_gather | solution.py:59
  58.5 2.4 copy-start.1
  147.2 47.8 %copy-start.4 = (f32[1,128,512]{2,1,0:T(8,128)S(1)}, f32[1,128,512]{2,1,0:T(8,128)}, u32[]{:S(2)}) copy-start(f32[1,128,512]{2,1,0:T(8,128)} %param.8) | copy-start | bytes 786436
  198.1 1.8 copy-start.5
  198.1 2.0 copy-start.6
  198.1 2.0 copy-start.7
  198.1 206.3 %all-reduce.4.cloned.1.call-start = ((), (), s32[]{:S(2)}) async-start(), calls=%async_computation.1 | async-start | bytes 2097152 | tf_op jit(solution)/shard_map/psum | solution.py:98
  254.3 20.6 %collective-permute-start = (f32[4,128,128]{2,0,1:T(4,128)S(1)}, f32[4,128,128]{2,0,1:T(4,128)S(1)}, u32[]{:S(2)}, u32[]{:S(2)}) collective-permute-start(f32[4,128,128]{2,0,1:T(4,128)S(1)} %fusion.73), channel_id=1, source_target_pairs={{0,16},{16,0},{32,48},{48,32},{64,80},{80,64},{96,112},{112,96},{1... | collective-permute-start | bytes 786440 | tf_op jit(solution)/shard_map/ppermute | solution.py:10
  257.3 27.1 %collective-permute-start.1 = (f32[4,128,128]{2,0,1:T(4,128)S(1)}, f32[4,128,128]{2,0,1:T(4,128)S(1)}, u32[]{:S(2)}, u32[]{:S(2)}) collective-permute-start(f32[4,128,128]{2,0,1:T(4,128)S(1)} %fusion.76), channel_id=1, source_target_pairs={{0,32},{16,48},{32,0},{48,16},{64,96},{80,112},{96,64},{112,80},{1... | collective-permute-start | bytes 786440 | tf_op jit(solution)/shard_map/ppermute | solution.py:10
  261.9 22.6 %collective-permute-start.2 = (f32[4,128,128]{2,0,1:T(4,128)S(1)}, f32[4,128,128]{2,0,1:T(4,128)S(1)}, u32[]{:S(2)}, u32[]{:S(2)}) collective-permute-start(f32[4,128,128]{2,0,1:T(4,128)S(1)} %fusion.79), channel_id=1, source_target_pairs={{0,64},{16,80},{32,96},{48,112},{64,0},{80,16},{96,32},{112,48},{1... | collective-permute-start | bytes 786440 | tf_op jit(solution)/shard_map/ppermute | solution.py:10
  266.7 17.7 %collective-permute-start.3 = (f32[4,128,128]{2,0,1:T(4,128)S(1)}, f32[4,128,128]{2,0,1:T(4,128)S(1)}, u32[]{:S(2)}, u32[]{:S(2)}) collective-permute-start(f32[4,128,128]{2,0,1:T(4,128)S(1)} %fusion.82), channel_id=1, source_target_pairs={{0,128},{16,144},{32,160},{48,176},{64,192},{80,208},{96,224},{112... | collective-permute-start | bytes 786440 | tf_op jit(solution)/shard_map/ppermute | solution.py:10
  270.3 14.2 %collective-permute-start.4 = (f32[4,128,128]{2,0,1:T(4,128)S(1)}, f32[4,128,128]{2,0,1:T(4,128)S(1)}, u32[]{:S(2)}, u32[]{:S(2)}) collective-permute-start(f32[4,128,128]{2,0,1:T(4,128)S(1)} %fusion.85), channel_id=1, source_target_pairs={{0,256},{16,272},{32,288},{48,304},{64,320},{80,336},{96,352},{112... | collective-permute-start | bytes 786440 | tf_op jit(solution)/shard_map/ppermute | solution.py:10
  286.7 1.0 copy-start.2
  404.4 1.7 copy-start
  406.3 1.0 copy-start.3
Sparse Core Ops, SparseCore 0:
  10.7 47.7 all-gather.5
  198.2 50.7 all-gather.3
  287.9 116.4 all-reduce.3
where the time goes:
time: 567 us; the launch traced here: 558 us
  other arithmetic  242 us (43%)
  waiting for transfers between devices  221 us (39%)
  local copies, waits for them, and re-layouts  33.7 us (6%)
  matrix products  21.9 us (4%)
  between operations  20.2 us (4%)
  starting transfers between devices  18.7 us (3%)
    psum x1, waiting for transfers between devices, per_device(): anc_pivot = lax.psum(contribution, 'front')  114 us
    another operation x15, other arithmetic, per_device(): anc_lower = jnp.linalg.cholesky(anc_pivot)  79.5 us
    another operation x14, other arithmetic, per_device(): lower = jnp.linalg.cholesky(pivot)  79 us
    all_gather x1, waiting for transfers between devices, per_device(): pivot = lax.all_gather(child_pivot[0], 'front', axis=0, tiled=True)  49.6 us
    all_gather x1, waiting for transfers between devices, per_device(): lax.all_gather(panel, 'front', axis=0, tiled=True)  47.6 us
    another operation x4, other arithmetic, per_device(): lax.linalg.triangular_solve(lower, child_panel[0], left_side=False, lower...  41.3 us
    another operation x2, other arithmetic, per_device(): lax.linalg.triangular_solve(anc_lower, assembled, left_side=False, lower=...  40.5 us
    ppermute x5, starting transfers between devices, swapped(): return lax.ppermute(value, axis, pairs)  18.6 us
  transfers between devices with their start and end apart: 8, of which 4 were waited for; matrix products, arithmetic and copies ran while one was open for 1% of the time, Pallas kernels for 0%

commit v1 on v0

--- a/solution.py
+++ b/solution.py
@@ -2,6 +2,7 @@
 import jax.numpy as jnp
 from jax import lax
 from jax.sharding import PartitionSpec as P
+from jax.lax import all_gather
 
 
 def swapped(value, axis, distance):
@@ -95,7 +96,11 @@
     contribution = lax.dynamic_update_slice_in_dim(
         jnp.zeros((width, width), jnp.float32), top_rows, owner_pos * block, 0
     )
-    anc_pivot = lax.psum(contribution, "front")
+
+    def ticks_test(field_in):
+        return jnp.sum(all_gather(field_in, axis_name="front"), 0)
+
+    anc_pivot = ticks_test(contribution)
     anc_lower = jnp.linalg.cholesky(anc_pivot)
     solved = lax.linalg.triangular_solve(
         anc_lower, assembled, left_side=False, lower=True, transpose_a=True

time: 567 us -> 549 us (0.968)
  waiting for transfers between devices: 221 us -> 204 us
  other arithmetic: 242 us -> 250 us
  local copies, waits for them, and re-layouts: 33.7 us -> 27.5 us
    psum x1 -> x0, waiting for transfers between devices: 114 us -> none  [per_device(): anc_pivot = lax.psum(contribution, 'front')]
    all_gather x0 -> x1, waiting for transfers between devices: none -> 96 us  [ticks_test(): return jnp.sum(all_gather(field_in, axis_name='front'), 0)]
    reduce_sum x0 -> x1, other arithmetic: none -> 7.91 us  [ticks_test(): return jnp.sum(all_gather(field_in, axis_name='front'), 0)]
    another operation x40 -> x27, local copies, waits for them, and re-layouts: 16.8 us -> 16.4 us
where the time goes in v1:
time: 549 us; the launch traced here: 540 us
  other arithmetic  250 us (46%)
  waiting for transfers between devices  204 us (37%)
  local copies, waits for them, and re-layouts  27.5 us (5%)
  between operations  20.1 us (4%)
  matrix products  19.1 us (3%)
  starting transfers between devices  18.7 us (3%)
    all_gather x1, waiting for transfers between devices, ticks_test(): return jnp.sum(all_gather(field_in, axis_name='front'), 0)  96 us
    another operation x15, other arithmetic, per_device(): anc_lower = jnp.linalg.cholesky(anc_pivot)  79.3 us
    another operation x14, other arithmetic, per_device(): lower = jnp.linalg.cholesky(pivot)  78.6 us
    all_gather x1, waiting for transfers between devices, per_device(): pivot = lax.all_gather(child_pivot[0], 'front', axis=0, tiled=True)  49.6 us
    all_gather x1, waiting for transfers between devices, per_device(): lax.all_gather(panel, 'front', axis=0, tiled=True)  49.2 us
    another operation x4, other arithmetic, per_device(): lax.linalg.triangular_solve(lower, child_panel[0], left_side=False, lower...  40.7 us
    another operation x2, other arithmetic, per_device(): lax.linalg.triangular_solve(anc_lower, assembled, left_side=False, lower=...  40.6 us
    ppermute x5, starting transfers between devices, swapped(): return lax.ppermute(value, axis, pairs)  18.6 us
  transfers between devices with their start and end apart: 8, of which 4 were waited for; matrix products, arithmetic and copies ran while one was open for 1% of the time, Pallas kernels for 0%

profile of v1, /device:TPU:1, one launch (start us, length us, event | category | flops | bytes accessed | tf_op | source)
XLA Modules:
  0.0 540.0 jit_solution(6522058480766709280)
XLA Ops:
  7.2 1.5 copy.65
  8.8 49.6 %all-gather.9.cloned.1.call-done = f32[1,512,512]{2,0,1:T(1,128)} async-done(((f32[1,32,512]{2,0,1:T(1,128)}), f32[1,512,512]{2,0,1:T(1,128)}) %all-gather.9.cloned.1.call-update) | async-done | bytes 1048592 | tf_op jit(solution)/shard_map/all_gather | solution.py:54
  58.5 2.4 copy.66
  61.2 11.7 %cholesky.286 = f32[128,128]{1,0:T(8,128)S(1)} custom-call(f32[128,128]{1,0:T(8,128)S(1)} %cholesky.426), custom_call_target="Cholesky" | custom-call | tf_op jit(solution)/shard_map/jit(cholesky)/cholesky | solution.py:55
  73.0 9.8 %custom-call.31 = f32[1,128,128]{1,2,0:T(8,128)S(1)} custom-call(f32[1,128,128]{2,1,0:T(8,128)S(1)} %get-tuple-element.91), custom_call_target="InvertDiagBlocksLowerTriangular" | custom-call | tf_op jit(solution)/shard_map/jit(cholesky)/cholesky | solution.py:55
  83.5 11.7 %cholesky.305 = f32[128,128]{1,0:T(8,128)S(1)} custom-call(f32[128,128]{1,0:T(8,128)S(1)} %cholesky.430), custom_call_target="Cholesky" | custom-call | tf_op jit(solution)/shard_map/jit(cholesky)/cholesky | solution.py:55
  95.3 10.0 %custom-call.32 = f32[1,128,128]{1,2,0:T(8,128)S(1)} custom-call(f32[1,128,128]{2,1,0:T(8,128)S(1)} %get-tuple-element.88), custom_call_target="InvertDiagBlocksLowerTriangular" | custom-call | tf_op jit(solution)/shard_map/jit(cholesky)/cholesky | solution.py:55
  105.9 11.7 %cholesky.326 = f32[128,128]{1,0:T(8,128)S(1)} custom-call(f32[128,128]{1,0:T(8,128)S(1)} %cholesky.435), custom_call_target="Cholesky" | custom-call | tf_op jit(solution)/shard_map/jit(cholesky)/cholesky | solution.py:55
  117.7 9.8 %custom-call.33 = f32[1,128,128]{1,2,0:T(8,128)S(1)} custom-call(f32[1,128,128]{2,1,0:T(8,128)S(1)} %get-tuple-element.85), custom_call_target="InvertDiagBlocksLowerTriangular" | custom-call | tf_op jit(solution)/shard_map/jit(cholesky)/cholesky | solution.py:55
  128.1 11.7 %cholesky.343 = f32[128,128]{1,0:T(8,128)S(1)} custom-call(f32[128,128]{1,0:T(8,128)S(1)} %convolution_subtract_fusion.11), custom_call_target="Cholesky" | custom-call | tf_op jit(solution)/shard_map/jit(cholesky)/cholesky | solution.py:55
  139.9 0.6 compare_reduce_fusion.10
  140.5 0.7 compare_reduce_fusion.9
  141.2 0.6 compare_reduce_fusion.11
  144.8 8.0 %while.2 = (s32[]{:T(128)}, f32[512,512]{1,0:T(8,128)S(1)}, s32[4,2]{0,1:T(2,128)S(1)}, f32[4,128,128]{2,1,0:T(8,128)S(1)}, s32[]{:T(128)}) while((s32[]{:T(128)}, f32[512,512]{1,0:T(8,128)S(1)}, s32[4,2]{0,1:T(2,128)S(1)}, f32[4,128,128]{2,1,0:T(8,128)S(1)}, s32[]{:T(128)}) %tuple.69), condition=%wide.while_cond, body=%wide.while_body.sunk | while | flops 2 | bytes 131189 | solution.py:57
  145.4 1.4 bitcast_dynamic-update-slice_fusion.9
  147.4 1.4 bitcast_dynamic-update-slice_fusion.9
  149.4 1.4 bitcast_dynamic-update-slice_fusion.9
  151.4 1.4 bitcast_dynamic-update-slice_fusion.9
  152.8 39.7 %custom-call.26 = f32[4,128,128]{1,2,0:T(8,128)S(1)} custom-call(f32[4,128,128]{2,1,0:T(8,128)S(1)} %get-tuple-element.11), custom_call_target="InvertDiagBlocksLowerTriangular" | custom-call | tf_op jit(solution)/shard_map/triangular_solve | solution.py:57
  195.0 0.7 pad_maximum_fusion
  197.5 49.2 %all-gather.5.cloned.1.call-done = f32[2048,512]{0,1:T(8,128)} async-done(((f32[128,512]{0,1:T(8,128)}), f32[2048,512]{0,1:T(8,128)}) %all-gather.5.cloned.1.call-update) | async-done | bytes 4194320 | tf_op jit(solution)/shard_map/all_gather | solution.py:60
  246.7 4.5 convolution_bitcast_fusion
  251.9 2.6 collective-permute-start
  254.9 4.0 collective-permute-start.1
  259.5 4.4 collective-permute-start.2
  264.4 3.1 collective-permute-start.3
  268.0 4.5 collective-permute-start.4
  272.5 9.5 %collective-permute-done.1 = f32[4,128,128]{2,0,1:T(4,128)S(1)} collective-permute-done((f32[4,128,128]{2,0,1:T(4,128)S(1)}, f32[4,128,128]{2,0,1:T(4,128)S(1)}, u32[]{:S(2)}, u32[]{:S(2)}) %collective-permute-start.1) | collective-permute-done | bytes 262176 | tf_op jit(solution)/shard_map/ppermute | solution.py:11
  282.2 1.2 convolution_bitcast_fusion.1
  283.6 1.0 copy-done.4
  285.0 1.0 copy-done.1
  286.0 0.8 copy.75
  286.9 0.6 dynamic-slice_bitcast_fusion
  287.5 96.0 %all-gather.7.cloned.1.call-done = f32[16,512,512]{2,1,0:T(8,128)} async-done(((f32[1,512,512]{2,1,0:T(8,128)}), f32[16,512,512]{2,1,0:T(8,128)}) %all-gather.7.cloned.1.call-update) | async-done | bytes 16777232 | tf_op jit(solution)/shard_map/all_gather | solution.py:101
  383.5 7.9 %reduce_sum.79 = f32[512,512]{1,0:T(8,128)S(1)} reduce(f32[16,512,512]{2,1,0:T(8,128)} %all-gather.7.cloned.1.call-done, f32[]{:T(128)} %constant.143.clone.1), dimensions={0}, to_apply=%region_15.17 | reduce | flops 3932160 | bytes 17825796 | tf_op jit(solution)/shard_map/reduce_sum | solution.py:101
  392.0 1.0 copy-done.2
  392.9 11.7 %cholesky.358 = f32[128,128]{1,0:T(8,128)S(1)} custom-call(f32[128,128]{1,0:T(8,128)S(1)} %cholesky.439), custom_call_target="Cholesky" | custom-call | tf_op jit(solution)/shard_map/jit(cholesky)/cholesky | solution.py:104
  404.8 9.8 %custom-call.34 = f32[1,128,128]{1,2,0:T(8,128)S(1)} custom-call(f32[1,128,128]{2,1,0:T(8,128)S(1)} %get-tuple-element.81), custom_call_target="InvertDiagBlocksLowerTriangular" | custom-call | tf_op jit(solution)/shard_map/jit(cholesky)/cholesky | solution.py:104
  415.3 11.9 %cholesky.377 = f32[128,128]{1,0:T(8,128)S(1)} custom-call(f32[128,128]{1,0:T(8,128)S(1)} %cholesky.443), custom_call_target="Cholesky" | custom-call | tf_op jit(solution)/shard_map/jit(cholesky)/cholesky | solution.py:104
  427.3 9.8 %custom-call.35 = f32[1,128,128]{1,2,0:T(8,128)S(1)} custom-call(f32[1,128,128]{2,1,0:T(8,128)S(1)} %get-tuple-element.78), custom_call_target="InvertDiagBlocksLowerTriangular" | custom-call | tf_op jit(solution)/shard_map/jit(cholesky)/cholesky | solution.py:104
  437.8 11.7 %cholesky.398 = f32[128,128]{1,0:T(8,128)S(1)} custom-call(f32[128,128]{1,0:T(8,128)S(1)} %cholesky.448), custom_call_target="Cholesky" | custom-call | tf_op jit(solution)/shard_map/jit(cholesky)/cholesky | solution.py:104
  449.5 9.8 %custom-call.36 = f32[1,128,128]{1,2,0:T(8,128)S(1)} custom-call(f32[1,128,128]{2,1,0:T(8,128)S(1)} %get-tuple-element.75), custom_call_target="InvertDiagBlocksLowerTriangular" | custom-call | tf_op jit(solution)/shard_map/jit(cholesky)/cholesky | solution.py:104
  459.5 0.6 convolution_subtract_fusion.9
  460.2 11.7 %cholesky.415 = f32[128,128]{1,0:T(8,128)S(1)} custom-call(f32[128,128]{1,0:T(8,128)S(1)} %convolution_subtract_fusion.9), custom_call_target="Cholesky" | custom-call | tf_op jit(solution)/shard_map/jit(cholesky)/cholesky | solution.py:104
  471.9 0.6 compare_reduce_fusion.8
  472.6 0.7 compare_reduce_fusion.7
  473.3 0.6 compare_reduce_fusion.6
  473.9 0.7 compare_reduce_fusion.5
  477.1 1.2 fusion.4
  478.4 8.1 %while.3 = (s32[]{:T(128)}, f32[512,512]{1,0:T(8,128)S(1)}, s32[4,2]{0,1:T(2,128)S(1)}, f32[4,128,128]{2,1,0:T(8,128)S(1)}, s32[]{:T(128)}) while((s32[]{:T(128)}, f32[512,512]{1,0:T(8,128)S(1)}, s32[4,2]{0,1:T(2,128)S(1)}, f32[4,128,128]{2,1,0:T(8,128)S(1)}, s32[]{:T(128)}) %tuple.81), condition=%wide.while_cond.1, body=%wide.while_body.1.sunk | while | flops 2 | bytes 131189 | solution.py:105
  478.4 0.6 fusion.126
  479.0 1.3 bitcast_dynamic-update-slice_fusion.10
  480.5 0.6 fusion.126
  481.1 1.3 bitcast_dynamic-update-slice_fusion.10
  482.5 0.6 fusion.126
  483.1 1.3 bitcast_dynamic-update-slice_fusion.10
  484.6 0.6 fusion.126
  485.2 1.3 bitcast_dynamic-update-slice_fusion.10
  486.5 39.3 %custom-call.27 = f32[4,128,128]{1,2,0:T(8,128)S(1)} custom-call(f32[4,128,128]{2,1,0:T(8,128)S(1)} %get-tuple-element.19), custom_call_target="InvertDiagBlocksLowerTriangular" | custom-call | tf_op jit(solution)/shard_map/triangular_solve | solution.py:105
  526.3 0.6 convolution_subtract_fusion.1
  527.3 1.0 convolution_subtract_fusion
  528.7 1.5 convolution_subtract_fusion.2
  530.9 1.0 constant_dynamic-slice_fusion.2
  531.9 1.1 fusion.1
  (116 shorter events, 17.2 us)
Async XLA Ops:
  7.2 51.3 %all-gather.9.cloned.1.call-start = ((), (), s32[]{:S(2)}) async-start(), calls=%async_computation.2 | async-start | bytes 1114112 | tf_op jit(solution)/shard_map/all_gather | solution.py:54
  8.8 237.9 %all-gather.5.cloned.1.call-start = ((), (), s32[]{:S(2)}) async-start(), calls=%async_computation | async-start | bytes 4456448 | tf_op jit(solution)/shard_map/all_gather | solution.py:60
  58.5 2.4 copy-start
  144.5 48.1 %copy-start.5 = (f32[1,128,512]{2,1,0:T(8,128)S(1)}, f32[1,128,512]{2,1,0:T(8,128)}, u32[]{:S(2)}) copy-start(f32[1,128,512]{2,1,0:T(8,128)} %param.8) | copy-start | bytes 786436
  193.1 2.7 copy-start.6
  193.2 2.9 copy-start.7
  193.2 2.9 copy-start.8
  195.7 187.7 %all-gather.7.cloned.1.call-start = ((), (), s32[]{:S(2)}) async-start(), calls=%async_computation.1 | async-start | bytes 17825792 | tf_op jit(solution)/shard_map/all_gather | solution.py:101
  251.9 20.6 %collective-permute-start = (f32[4,128,128]{2,0,1:T(4,128)S(1)}, f32[4,128,128]{2,0,1:T(4,128)S(1)}, u32[]{:S(2)}, u32[]{:S(2)}) collective-permute-start(f32[4,128,128]{2,0,1:T(4,128)S(1)} %fusion.74), channel_id=1, source_target_pairs={{0,16},{16,0},{32,48},{48,32},{64,80},{80,64},{96,112},{112,96},{1... | collective-permute-start | bytes 786440 | tf_op jit(solution)/shard_map/ppermute | solution.py:11
  254.9 27.1 %collective-permute-start.1 = (f32[4,128,128]{2,0,1:T(4,128)S(1)}, f32[4,128,128]{2,0,1:T(4,128)S(1)}, u32[]{:S(2)}, u32[]{:S(2)}) collective-permute-start(f32[4,128,128]{2,0,1:T(4,128)S(1)} %fusion.77), channel_id=1, source_target_pairs={{0,32},{16,48},{32,0},{48,16},{64,96},{80,112},{96,64},{112,80},{1... | collective-permute-start | bytes 786440 | tf_op jit(solution)/shard_map/ppermute | solution.py:11
  259.5 22.6 %collective-permute-start.2 = (f32[4,128,128]{2,0,1:T(4,128)S(1)}, f32[4,128,128]{2,0,1:T(4,128)S(1)}, u32[]{:S(2)}, u32[]{:S(2)}) collective-permute-start(f32[4,128,128]{2,0,1:T(4,128)S(1)} %fusion.80), channel_id=1, source_target_pairs={{0,64},{16,80},{32,96},{48,112},{64,0},{80,16},{96,32},{112,48},{1... | collective-permute-start | bytes 786440 | tf_op jit(solution)/shard_map/ppermute | solution.py:11
  264.4 17.7 %collective-permute-start.3 = (f32[4,128,128]{2,0,1:T(4,128)S(1)}, f32[4,128,128]{2,0,1:T(4,128)S(1)}, u32[]{:S(2)}, u32[]{:S(2)}) collective-permute-start(f32[4,128,128]{2,0,1:T(4,128)S(1)} %fusion.83), channel_id=1, source_target_pairs={{0,128},{16,144},{32,160},{48,176},{64,192},{80,208},{96,224},{112... | collective-permute-start | bytes 786440 | tf_op jit(solution)/shard_map/ppermute | solution.py:11
  268.0 14.2 %collective-permute-start.4 = (f32[4,128,128]{2,0,1:T(4,128)S(1)}, f32[4,128,128]{2,0,1:T(4,128)S(1)}, u32[]{:S(2)}, u32[]{:S(2)}) collective-permute-start(f32[4,128,128]{2,0,1:T(4,128)S(1)} %fusion.86), channel_id=1, source_target_pairs={{0,256},{16,272},{32,288},{48,304},{64,320},{80,336},{96,352},{112... | collective-permute-start | bytes 786440 | tf_op jit(solution)/shard_map/ppermute | solution.py:11
  283.4 1.2 copy-start.4
  285.0 1.0 copy-start.1
  392.0 1.0 copy-start.2
  392.9 21.7 %copy-start.3 = (f32[512,512]{1,0:T(8,128)S(1)}, f32[512,512]{1,0:T(8,128)}, u32[]{:S(2)}) copy-start(f32[512,512]{1,0:T(8,128)} %copy-done.2) | copy-start | bytes 3145732
Sparse Core Ops, SparseCore 0:
  10.7 47.7 all-gather.8
  195.8 50.8 all-gather.4
  286.1 97.2 all-gather.6
